TPU v7x, 32 devices: a whole 2x2x4 slice. The times are simulated.
32 devices in a mesh: row: 8 (over z, x), col: 4 (over y, core).
Axes of the slice: x: 2, y: 2, z: 4, core: 2. Of those that a mesh axis runs over, the one named last changes fastest.
Arguments:
- features: bfloat16 [8192, 256], P(('row', 'col')), may hold values from -6 to 6
- grad_out: bfloat16 [8192, 256], P(('row', 'col')), may hold values from -6 to 6
- degrees: int32 [8192], P(('row', 'col')), may hold values from 1 to 8236, as said below
- w_self: bfloat16 [256, 256], replicated, may hold values from -0.375 to 0.375
- w_neigh: bfloat16 [256, 256], replicated, may hold values from -0.375 to 0.375
- bias: float32 [256], replicated, may hold values from -4 to 4
- tile_slots: int32 [8, 4, 88], P('row', 'col'), may hold values from 0 to 127, as said below
- tile_count: int32 [8, 4], P('row', 'col'), may hold values from 22 to 88, as said below
- tile_masks: int32 [8, 4, 88, 16, 128], P('row', 'col'), may hold values from 0 to 255
Outputs:
- layer_out: bfloat16 [8192, 256], P(('row', 'col'))
- grad_in: bfloat16 [8192, 256], P(('row', 'col'))
- grad_w_self: float32 [256, 256], replicated
- grad_w_neigh: float32 [256, 256], replicated
Inputs may be any that keep to these rules, and one draw needn't show every extreme that they name: `tile_slots`: on each device the 88 slot numbers are distinct and rise; slot s names block row s % 8 of the device's row group and block column s // 8 of its panel. Only a device's first tile_count tiles are live; the others are ignored. Some device holds 88 live tiles. `degrees`: each node's degree is at least the number of ones in its row of A, and at least 1; some node has the largest degree.
All inputs are finite; a program needn't handle non-finite values.
Results may differ from a plain program's by a relative error of at most 0.014.
Values may be sent and summed in bfloat16 or wider, within the bound.
No kernel may reach another device: no remote copies, remote signals or barrier semaphores. Data moves between devices by JAX's collectives and lax.ppermute only.
A program may use at most 64 MiB of HBM per device.

v0:
```python
import math
import jax
import jax.numpy as jnp
from jax import lax
from jax.sharding import PartitionSpec as P

group_tiles = 8


def unpack_tiles(mask_words):
    shifts = jnp.arange(8, dtype=jnp.int32)
    bit_values = jnp.bitwise_and(
        jnp.right_shift(mask_words[:, :, None, :], shifts[None, None, :, None]), 1
    )
    return bit_values.reshape(mask_words.shape[0], mask_words.shape[1] * 8, mask_words.shape[2])


def tile_range(slot_ids, live_count, block_rows, low_column, high_column, tile_width):
    column_block = slot_ids // block_rows
    positions = jnp.arange(slot_ids.shape[0], dtype=jnp.int32)
    is_live = positions < live_count
    first_tile = jnp.sum(
        jnp.logical_and(is_live, (column_block + 1) * tile_width <= low_column).astype(jnp.int32)
    )
    last_tile = jnp.sum(
        jnp.logical_and(is_live, column_block * tile_width < high_column).astype(jnp.int32)
    )
    return (first_tile, last_tile)


def aggregate_piece(totals, panel_piece, first_row, slot_ids, live_count, mask_words):
    tile_width = mask_words.shape[2]
    block_rows = totals.shape[0] // tile_width
    piece_rows = panel_piece.shape[0]
    feature_width = panel_piece.shape[1]
    first_tile, last_tile = tile_range(
        slot_ids, live_count, block_rows, first_row, first_row + piece_rows, tile_width
    )
    margin = jnp.zeros((tile_width, feature_width), panel_piece.dtype)
    padded = jnp.concatenate([margin, panel_piece, margin], axis=0)
    group_count = (last_tile - first_tile + group_tiles - 1) // group_tiles
    within = jnp.arange(group_tiles, dtype=jnp.int32)
    tile_columns = jnp.arange(tile_width, dtype=jnp.int32)

    def aggregate_one_group(group_index, running):
        chosen = first_tile + group_index * group_tiles + within
        in_range = chosen < last_tile
        chosen = jnp.minimum(chosen, slot_ids.shape[0] - 1)
        chosen_slots = slot_ids[chosen]
        row_block = chosen_slots % block_rows
        column_block = chosen_slots // block_rows
        columns = column_block[:, None] * tile_width + tile_columns[None, :]
        keep_mask = in_range[:, None] & (columns >= first_row) & (columns < first_row + piece_rows)
        tile_bits = unpack_tiles(mask_words[chosen]) * keep_mask[:, :, None].astype(jnp.int32)
        offsets = column_block * tile_width - first_row + tile_width
        blocks = jax.vmap(lambda offset: lax.dynamic_slice_in_dim(padded, offset, tile_width, 0))(
            offsets
        )
        products = jnp.einsum(
            "gji,gjf->gif",
            tile_bits.astype(jnp.bfloat16),
            blocks,
            preferred_element_type=jnp.float32,
        )
        shaped = running.reshape(block_rows, tile_width, feature_width)
        return shaped.at[row_block].add(products).reshape(running.shape)

    return lax.fori_loop(0, group_count, aggregate_one_group, totals)


def spread_rows(first_row, row_count, slot_ids, live_count, mask_words, upward_rows):
    tile_width = mask_words.shape[2]
    block_rows = upward_rows.shape[0] // tile_width
    feature_width = upward_rows.shape[1]
    first_tile, last_tile = tile_range(
        slot_ids, live_count, block_rows, first_row, first_row + row_count, tile_width
    )
    first_block = first_row // tile_width
    upward_blocks = upward_rows.reshape(block_rows, tile_width, feature_width)
    group_count = (last_tile - first_tile + group_tiles - 1) // group_tiles
    within = jnp.arange(group_tiles, dtype=jnp.int32)

    def spread_one_group(group_index, running):
        chosen = first_tile + group_index * group_tiles + within
        in_range = chosen < last_tile
        chosen = jnp.minimum(chosen, slot_ids.shape[0] - 1)
        chosen_slots = slot_ids[chosen]
        row_block = chosen_slots % block_rows
        column_block = chosen_slots // block_rows
        tile_bits = unpack_tiles(mask_words[chosen]) * in_range[:, None, None].astype(jnp.int32)
        sources = upward_blocks[row_block]
        products = jnp.einsum(
            "gji,gif->gjf",
            tile_bits.astype(jnp.bfloat16),
            sources,
            preferred_element_type=jnp.float32,
        )
        return running.at[column_block - first_block].add(products)

    initial = jnp.zeros((row_count // tile_width, tile_width, feature_width), jnp.float32)
    partial_value = lax.fori_loop(0, group_count, spread_one_group, initial)
    return partial_value.reshape(row_count, feature_width)


def shards(features, grad_out, degrees, w_self, w_neigh, bias, tile_slots, tile_count, tile_masks):
    slot_ids = tile_slots[0, 0]
    live_count = tile_count[0, 0]
    mask_words = tile_masks[0, 0]
    node_rows, feature_width = features.shape
    group_size = node_rows * lax.axis_size("col")
    initial = jnp.zeros((group_size, feature_width), jnp.float32)
    panel = lax.all_gather(features, "row", axis=0, tiled=True)
    partial_value = aggregate_piece(initial, panel, 0, slot_ids, live_count, mask_words)
    summed = lax.psum_scatter(
        partial_value.astype(jnp.bfloat16), "col", scatter_dimension=0, tiled=True
    ).astype(jnp.float32)
    scale_degree = degrees.astype(jnp.float32)[:, None]
    mean_rows = (summed / scale_degree).astype(jnp.bfloat16)
    preact = jnp.dot(features, w_self, preferred_element_type=jnp.float32)
    preact = preact + jnp.dot(mean_rows, w_neigh, preferred_element_type=jnp.float32) + bias
    sigmoid_values = jax.nn.sigmoid(preact)
    layer_out = (preact * sigmoid_values).astype(jnp.bfloat16)
    grad_preact = (
        grad_out.astype(jnp.float32) * sigmoid_values * (1.0 + preact * (1.0 - sigmoid_values))
    ).astype(jnp.bfloat16)
    contract_rows = (((0,), (0,)), ((), ()))
    contract_cols = (((1,), (1,)), ((), ()))
    grad_self = lax.dot_general(
        features, grad_preact, contract_rows, preferred_element_type=jnp.float32
    )
    grad_neigh = lax.dot_general(
        mean_rows, grad_preact, contract_rows, preferred_element_type=jnp.float32
    )
    grad_self, grad_neigh = lax.psum((grad_self, grad_neigh), ("row", "col"))
    grad_scale = 1.0 / math.sqrt(node_rows * lax.axis_size("row") * lax.axis_size("col"))
    upward = lax.dot_general(
        grad_preact, w_neigh, contract_cols, preferred_element_type=jnp.float32
    )
    upward = (upward / scale_degree).astype(jnp.bfloat16)
    upward_rows = lax.all_gather(upward, "col", axis=0, tiled=True)
    panel_size = node_rows * lax.axis_size("row")
    neighbor_grad = lax.psum_scatter(
        spread_rows(0, panel_size, slot_ids, live_count, mask_words, upward_rows).astype(
            jnp.bfloat16
        ),
        "row",
        scatter_dimension=0,
        tiled=True,
    ).astype(jnp.float32)
    self_grad = lax.dot_general(
        grad_preact, w_self, contract_cols, preferred_element_type=jnp.float32
    )
    grad_in = (self_grad + neighbor_grad).astype(jnp.bfloat16)
    return (layer_out, grad_in, grad_self * grad_scale, grad_neigh * grad_scale)


def solution(mesh):
    placed = (
        P(("row", "col"), None),
        P(("row", "col"), None),
        P(("row", "col")),
        P(),
        P(),
        P(),
        P("row", "col", None),
        P("row", "col"),
        P("row", "col", None, None, None),
    )
    return jax.shard_map(
        shards,
        mesh=mesh,
        in_specs=placed,
        out_specs=(P(("row", "col"), None), P(("row", "col"), None), P(), P()),
        check_vma=False,
    )
```

profile of v0, /device:TPU:0, one launch (start us, length us, event | category | flops | bytes accessed | tf_op | source)
XLA Modules:
  0.0 546.3 jit_solution(3008152126363309649)
XLA Ops:
  11.3 41.9 %all-gather.2.cloned.1.call-done = bf16[2048,256]{1,0:T(8,128)(2,1)} async-done(((bf16[256,256]{1,0:T(8,128)(2,1)}), bf16[2048,256]{1,0:T(8,128)(2,1)}) %all-gather.2.cloned.1.call-update) | async-done | bytes 1048592 | tf_op jit(solution)/shard_map/all_gather | solution.py:112
  53.2 2.3 pad_maximum_fusion
  55.6 253.4 %while.30 = (s32[]{:T(128)}, f32[1024,256]{1,0:T(8,128)S(1)}, s32[]{:T(128)}, s32[]{:T(128)}, s32[88]{0:T(128)S(1)}, /*index=5*/s32[88,16,128]{2,1,0:T(8,128)}, ...) while((s32[]{:T(128)}, f32[1024,256]{1,0:T(8,128)S(1)}, ...), condition=%wide.region_4.5_spmd.clone, body=%wide.region_2.4_spmd.clone.sunk | while | flops 67902872 | bytes 5061454 | solution.py:68
  57.0 17.3 %while.32 = (s32[]{:T(128)}, bf16[2304,256]{1,0:T(8,128)(2,1)}, s32[8,2]{0,1:T(2,128)S(1)}, bf16[8,128,256]{2,1,0:T(8,128)(2,1)S(1)}, s32[]{:T(128)}) while((s32[]{:T(128)}, bf16[2304,256]{1,0:T(8,128)(2,1)}, s32[8,2]{0,1:T(2,128)S(1)}, bf16[8,128,256]{2,1,0:T(8,128)(2,1)S(1)}, s32[]{:T(128)}) %tuple.84), condition=%wide.while_cond, body=%wide.while_body.sunk | while | flops 2 | bytes 131177 | solution.py:56
  57.6 1.6 bitcast_dynamic-update-slice_fusion.2
  59.8 1.6 bitcast_dynamic-update-slice_fusion.2
  61.9 1.6 bitcast_dynamic-update-slice_fusion.2
  64.1 1.6 bitcast_dynamic-update-slice_fusion.2
  68.4 1.6 bitcast_dynamic-update-slice_fusion.2
  70.6 1.6 bitcast_dynamic-update-slice_fusion.2
  75.0 1.7 gather_fusion.4
  80.0 17.3 %while.32 = (s32[]{:T(128)}, bf16[2304,256]{1,0:T(8,128)(2,1)}, s32[8,2]{0,1:T(2,128)S(1)}, bf16[8,128,256]{2,1,0:T(8,128)(2,1)S(1)}, s32[]{:T(128)}) while((s32[]{:T(128)}, bf16[2304,256]{1,0:T(8,128)(2,1)}, s32[8,2]{0,1:T(2,128)S(1)}, bf16[8,128,256]{2,1,0:T(8,128)(2,1)S(1)}, s32[]{:T(128)}) %tuple.84), condition=%wide.while_cond, body=%wide.while_body.sunk | while | flops 2 | bytes 131177 | solution.py:56
  80.6 1.6 bitcast_dynamic-update-slice_fusion.2
  82.8 1.6 bitcast_dynamic-update-slice_fusion.2
  98.1 1.7 gather_fusion.4
  103.1 17.3 %while.32 = (s32[]{:T(128)}, bf16[2304,256]{1,0:T(8,128)(2,1)}, s32[8,2]{0,1:T(2,128)S(1)}, bf16[8,128,256]{2,1,0:T(8,128)(2,1)S(1)}, s32[]{:T(128)}) while((s32[]{:T(128)}, bf16[2304,256]{1,0:T(8,128)(2,1)}, s32[8,2]{0,1:T(2,128)S(1)}, bf16[8,128,256]{2,1,0:T(8,128)(2,1)S(1)}, s32[]{:T(128)}) %tuple.84), condition=%wide.while_cond, body=%wide.while_body.sunk | while | flops 2 | bytes 131177 | solution.py:56
  121.1 1.7 gather_fusion.4
  126.1 17.3 %while.32 = (s32[]{:T(128)}, bf16[2304,256]{1,0:T(8,128)(2,1)}, s32[8,2]{0,1:T(2,128)S(1)}, bf16[8,128,256]{2,1,0:T(8,128)(2,1)S(1)}, s32[]{:T(128)}) while((s32[]{:T(128)}, bf16[2304,256]{1,0:T(8,128)(2,1)}, s32[8,2]{0,1:T(2,128)S(1)}, bf16[8,128,256]{2,1,0:T(8,128)(2,1)S(1)}, s32[]{:T(128)}) %tuple.84), condition=%wide.while_cond, body=%wide.while_body.sunk | while | flops 2 | bytes 131177 | solution.py:56
  144.2 1.7 gather_fusion.4
  149.2 17.3 %while.32 = (s32[]{:T(128)}, bf16[2304,256]{1,0:T(8,128)(2,1)}, s32[8,2]{0,1:T(2,128)S(1)}, bf16[8,128,256]{2,1,0:T(8,128)(2,1)S(1)}, s32[]{:T(128)}) while((s32[]{:T(128)}, bf16[2304,256]{1,0:T(8,128)(2,1)}, s32[8,2]{0,1:T(2,128)S(1)}, bf16[8,128,256]{2,1,0:T(8,128)(2,1)S(1)}, s32[]{:T(128)}) %tuple.84), condition=%wide.while_cond, body=%wide.while_body.sunk | while | flops 2 | bytes 131177 | solution.py:56
  167.2 1.7 gather_fusion.4
  172.2 17.3 %while.32 = (s32[]{:T(128)}, bf16[2304,256]{1,0:T(8,128)(2,1)}, s32[8,2]{0,1:T(2,128)S(1)}, bf16[8,128,256]{2,1,0:T(8,128)(2,1)S(1)}, s32[]{:T(128)}) while((s32[]{:T(128)}, bf16[2304,256]{1,0:T(8,128)(2,1)}, s32[8,2]{0,1:T(2,128)S(1)}, bf16[8,128,256]{2,1,0:T(8,128)(2,1)S(1)}, s32[]{:T(128)}) %tuple.84), condition=%wide.while_cond, body=%wide.while_body.sunk | while | flops 2 | bytes 131177 | solution.py:56
  190.2 1.7 gather_fusion.4
  195.2 17.3 %while.32 = (s32[]{:T(128)}, bf16[2304,256]{1,0:T(8,128)(2,1)}, s32[8,2]{0,1:T(2,128)S(1)}, bf16[8,128,256]{2,1,0:T(8,128)(2,1)S(1)}, s32[]{:T(128)}) while((s32[]{:T(128)}, bf16[2304,256]{1,0:T(8,128)(2,1)}, s32[8,2]{0,1:T(2,128)S(1)}, bf16[8,128,256]{2,1,0:T(8,128)(2,1)S(1)}, s32[]{:T(128)}) %tuple.84), condition=%wide.while_cond, body=%wide.while_body.sunk | while | flops 2 | bytes 131177 | solution.py:56
  213.3 1.7 gather_fusion.4
  218.3 17.3 %while.32 = (s32[]{:T(128)}, bf16[2304,256]{1,0:T(8,128)(2,1)}, s32[8,2]{0,1:T(2,128)S(1)}, bf16[8,128,256]{2,1,0:T(8,128)(2,1)S(1)}, s32[]{:T(128)}) while((s32[]{:T(128)}, bf16[2304,256]{1,0:T(8,128)(2,1)}, s32[8,2]{0,1:T(2,128)S(1)}, bf16[8,128,256]{2,1,0:T(8,128)(2,1)S(1)}, s32[]{:T(128)}) %tuple.84), condition=%wide.while_cond, body=%wide.while_body.sunk | while | flops 2 | bytes 131177 | solution.py:56
  236.3 1.7 gather_fusion.4
  241.3 17.3 %while.32 = (s32[]{:T(128)}, bf16[2304,256]{1,0:T(8,128)(2,1)}, s32[8,2]{0,1:T(2,128)S(1)}, bf16[8,128,256]{2,1,0:T(8,128)(2,1)S(1)}, s32[]{:T(128)}) while((s32[]{:T(128)}, bf16[2304,256]{1,0:T(8,128)(2,1)}, s32[8,2]{0,1:T(2,128)S(1)}, bf16[8,128,256]{2,1,0:T(8,128)(2,1)S(1)}, s32[]{:T(128)}) %tuple.84), condition=%wide.while_cond, body=%wide.while_body.sunk | while | flops 2 | bytes 131177 | solution.py:56
  259.3 1.7 gather_fusion.4
  264.3 17.3 %while.32 = (s32[]{:T(128)}, bf16[2304,256]{1,0:T(8,128)(2,1)}, s32[8,2]{0,1:T(2,128)S(1)}, bf16[8,128,256]{2,1,0:T(8,128)(2,1)S(1)}, s32[]{:T(128)}) while((s32[]{:T(128)}, bf16[2304,256]{1,0:T(8,128)(2,1)}, s32[8,2]{0,1:T(2,128)S(1)}, bf16[8,128,256]{2,1,0:T(8,128)(2,1)S(1)}, s32[]{:T(128)}) %tuple.84), condition=%wide.while_cond, body=%wide.while_body.sunk | while | flops 2 | bytes 131177 | solution.py:56
  282.4 1.7 gather_fusion.4
  287.4 17.3 %while.32 = (s32[]{:T(128)}, bf16[2304,256]{1,0:T(8,128)(2,1)}, s32[8,2]{0,1:T(2,128)S(1)}, bf16[8,128,256]{2,1,0:T(8,128)(2,1)S(1)}, s32[]{:T(128)}) while((s32[]{:T(128)}, bf16[2304,256]{1,0:T(8,128)(2,1)}, s32[8,2]{0,1:T(2,128)S(1)}, bf16[8,128,256]{2,1,0:T(8,128)(2,1)S(1)}, s32[]{:T(128)}) %tuple.84), condition=%wide.while_cond, body=%wide.while_body.sunk | while | flops 2 | bytes 131177 | solution.py:56
  305.4 1.7 gather_fusion.4
  310.2 20.3 %reduce-scatter.3.cloned.1.call-done = bf16[256,256]{1,0:T(8,128)(2,1)} async-done(((bf16[1024,256]{1,0:T(8,128)(2,1)}), bf16[256,256]{1,0:T(8,128)(2,1)}) %reduce-scatter.3.cloned.1.call-update) | async-done | bytes 131088 | tf_op jit(solution)/shard_map/reduce_scatter | solution.py:114
  330.5 2.0 multiply_convert_fusion
  333.6 6.6 %all_gather.7 = bf16[1024,256]{1,0:T(8,128)(2,1)S(1)} all-gather(bf16[256,256]{1,0:T(8,128)(2,1)S(1)} %fusion.42), channel_id=1, replica_groups=mesh['row'=8,'col'=4] {'col'}, dimensions={0}, use_global_device_ids=true | all-gather | bytes 655360 | tf_op jit(solution)/shard_map/all_gather | solution.py:140
  341.3 1.6 broadcast_in_dim.8
  342.8 87.3 %while.31 = (s32[]{:T(128)}, f32[16,128,256]{2,1,0:T(8,128)}, s32[]{:T(128)}, s32[]{:T(128)}, s32[88]{0:T(128)S(1)}, /*index=5*/s32[88,16,128]{2,1,0:T(8,128)}, ...) while((s32[]{:T(128)}, f32[16,128,256]{2,1,0:T(8,128)}, s32[]{:T(128)}, ...), condition=%wide.region_8.9_spmd.clone, body=%wide.region_6.8_spmd.clone.sunk | while | flops 67897608 | bytes 5974609 | solution.py:101
  345.5 1.7 gather_fusion.2
  347.5 3.3 scatter_fusion
  353.4 1.7 gather_fusion.2
  355.5 3.1 scatter_fusion
  361.2 1.7 gather_fusion.2
  363.2 3.1 scatter_fusion
  369.0 1.7 gather_fusion.2
  371.0 3.3 scatter_fusion
  376.9 1.7 gather_fusion.2
  379.0 3.1 scatter_fusion
  384.7 1.7 gather_fusion.2
  386.7 3.3 scatter_fusion
  392.7 1.7 gather_fusion.2
  394.7 3.4 scatter_fusion
  400.7 1.7 gather_fusion.2
  402.8 3.4 scatter_fusion
  408.8 1.7 gather_fusion.2
  410.8 3.2 scatter_fusion
  416.6 1.7 gather_fusion.2
  418.7 3.3 scatter_fusion
  424.6 1.7 gather_fusion.2
  426.6 3.5 scatter_fusion
  430.1 2.7 convert_element_type.88
  432.8 38.5 %all-reduce.4.cloned.1.call-done = (f32[256,256]{0,1:T(8,128)}, f32[256,256]{0,1:T(8,128)}) async-done(((f32[256,256]{0,1:T(8,128)}, f32[256,256]{0,1:T(8,128)}), (f32[256,256]{0,1:T(8,128)}, f32[256,256]{0,1:T(8,128)})) %all-reduce.4.cloned.1.call-update) | async-done | bytes 524304 | tf_op jit(solution)/shard_map/psum | solution.py:134
  474.1 63.9 %reduce-scatter.5.cloned.1.call-done = bf16[256,256]{1,0:T(8,128)(2,1)} async-done(((bf16[2048,256]{1,0:T(8,128)(2,1)}), bf16[256,256]{1,0:T(8,128)(2,1)}) %reduce-scatter.5.cloned.1.call-update) | async-done | bytes 131088 | tf_op jit(solution)/shard_map/reduce_scatter | solution.py:142
  538.0 1.8 fusion.41
  (545 shorter events, 245.6 us)
Async XLA Ops:
  7.2 323.3 %copy-start = (bf16[256,256]{1,0:T(8,128)(2,1)S(1)}, bf16[256,256]{1,0:T(8,128)(2,1)}, u32[]{:S(2)}) copy-start(bf16[256,256]{1,0:T(8,128)(2,1)} %param.17) | copy-start | bytes 393220
  7.2 48.4 %copy-start.1 = (s32[1,1,88]{2,1,0:T(1,128)S(1)}, s32[1,1,88]{2,1,0:T(1,128)}, u32[]{:S(2)}) copy-start(s32[1,1,88]{2,1,0:T(1,128)} %param.19) | copy-start | bytes 1060
  7.2 46.0 %all-gather.2.cloned.1.call-start = ((), (), s32[]{:S(2)}) async-start(), calls=%async_computation.2 | async-start | bytes 1179648 | tf_op jit(solution)/shard_map/all_gather | solution.py:112
  7.9 322.6 %reduce-scatter.3.cloned.1.call-start = ((), (), s32[]{:S(2)}) async-start(), calls=%async_computation.3 | async-start | bytes 655360 | tf_op jit(solution)/shard_map/reduce_scatter | solution.py:114
  309.0 1.0 copy-start.4
  309.0 1.0 copy-start.2
  309.0 1.0 copy-start.3
  309.0 21.5 %copy-start.5 = (bf16[256,256]{1,0:T(8,128)(2,1)S(1)}, bf16[256,256]{1,0:T(8,128)(2,1)}, u32[]{:S(2)}) copy-start(bf16[256,256]{1,0:T(8,128)(2,1)} %param.14) | copy-start | bytes 393220
  309.0 21.4 %copy-start.7 = (f32[256]{0:T(256)S(1)}, f32[256]{0:T(256)}, u32[]{:S(2)}) copy-start(f32[256]{0:T(256)} %param.18) | copy-start | bytes 3076
  309.9 161.4 %all-reduce.4.cloned.1.call-start = ((), (), s32[]{:S(2)}) async-start(), calls=%async_computation.5 | async-start | bytes 1048576 | tf_op jit(solution)/shard_map/psum | solution.py:134
  330.5 9.7 %copy-start.6 = (bf16[256,256]{1,0:T(8,128)(2,1)S(1)}, bf16[256,256]{1,0:T(8,128)(2,1)}, u32[]{:S(2)}) copy-start(bf16[256,256]{1,0:T(8,128)(2,1)} %reduce-scatter.3.cloned.1.call-done) | copy-start | bytes 393220
  341.2 196.7 %reduce-scatter.5.cloned.1.call-start = ((), (), s32[]{:S(2)}) async-start(), calls=%async_computation.4 | async-start | bytes 1179648 | tf_op jit(solution)/shard_map/reduce_scatter | solution.py:142
Sparse Core Ops, SparseCore 0:
  10.1 42.9 all-gather.1
  310.1 20.3 reduce-scatter.2
  341.3 129.9 all-reduce.3
  474.6 63.3 reduce-scatter.4
where the time goes:
time: 553 us; the launch traced here: 546 us
  local copies, waits for them, and re-layouts  251 us (45%)
  waiting for transfers between devices  165 us (30%)
  other arithmetic  72.9 us (13%)
  loops' own time  18.5 us (3%)
  matrix products  16.1 us (3%)
  between operations  15.8 us (3%)
  blocking collectives  6.59 us (1%)
    gather x264, local copies, waits for them, and re-layouts  188 us
    reduce_scatter x1, waiting for transfers between devices, shards(): lax.psum_scatter(spread_rows(0, panel_size, slot_ids, live_count, mask_wo...  63.9 us
    all_gather x1, waiting for transfers between devices, shards(): panel = lax.all_gather(features, 'row', axis=0, tiled=True)  41.9 us
    psum x1, waiting for transfers between devices, shards(): grad_self, grad_neigh = lax.psum((grad_self, grad_neigh), ('row', 'col'))  38.5 us
    scatter-add x11, other arithmetic, spread_one_group(): return running.at[column_block - first_block].add(products)  35.9 us
    reduce_scatter x1, waiting for transfers between devices, shards(): lax.psum_scatter(partial_value.astype(jnp.bfloat16), 'col', scatter_dimen...  20.3 us
    gather x11, local copies, waits for them, and re-layouts, spread_one_group(): mask_words[chosen]  18.3 us
    gather x11, local copies, waits for them, and re-layouts, aggregate_one_group(): mask_words[chosen]  18.3 us
  transfers between devices with their start and end apart: 4, of which 4 were waited for; matrix products, arithmetic and copies ran while one was open for 16% of the time, Pallas kernels for 0%

commit v1 on v0

--- a/solution.py
+++ b/solution.py
@@ -109,7 +109,16 @@
     node_rows, feature_width = features.shape
     group_size = node_rows * lax.axis_size("col")
     initial = jnp.zeros((group_size, feature_width), jnp.float32)
-    panel = lax.all_gather(features, "row", axis=0, tiled=True)
+    ways = lax.axis_size("row")
+    up = [(d, (d + 1) % ways) for d in range(ways)]
+    down = [(d, (d - 1) % ways) for d in range(ways)]
+    earlier, later = ([features], [features])
+    for _ in range(ways // 2):
+        earlier.append(lax.ppermute(earlier[-1], "row", up))
+    for _ in range((ways - 1) // 2):
+        later.append(lax.ppermute(later[-1], "row", down))
+    line = jnp.concatenate([*earlier[::-1], *later[1:]], axis=0)
+    panel = jnp.roll(line, (lax.axis_index("row") - ways // 2) * features.shape[0], axis=0)
     partial_value = aggregate_piece(initial, panel, 0, slot_ids, live_count, mask_words)
     summed = lax.psum_scatter(
         partial_value.astype(jnp.bfloat16), "col", scatter_dimension=0, tiled=True

time: 553 us -> 545 us (0.986)
  waiting for transfers between devices: 165 us -> 141 us
  starting transfers between devices: 0.16 us -> 17.4 us
    all_gather x1 -> x0, waiting for transfers between devices: 41.9 us -> none  [shards(): panel = lax.all_gather(features, 'row', axis=0, tiled=True)]
    ppermute x0 -> x7, starting transfers between devices: none -> 17.3 us  [the longest x3 14.2 us: shards(): later.append(lax.ppermute(later[-1], 'row', down))]
    ppermute x0 -> x7, waiting for transfers between devices: none -> 14.1 us  [the longest x4 12.4 us: shards(): earlier.append(lax.ppermute(earlier[-1], 'row', up))]
  transfers between devices with their start and end apart: 4 -> 10, of which waited for: 4 -> 8; matrix products, arithmetic and copies ran while one was open for 16% -> 16% of each run, Pallas kernels for 0% -> 0%
where the time goes in v1:
time: 545 us; the launch traced here: 538 us
  local copies, waits for them, and re-layouts  252 us (46%)
  waiting for transfers between devices  141 us (26%)
  other arithmetic  72 us (13%)
  starting transfers between devices  17.4 us (3%)
  loops' own time  17.3 us (3%)
  matrix products  16.1 us (3%)
  between operations  16 us (3%)
  blocking collectives  6.59 us (1%)
    gather x264, local copies, waits for them, and re-layouts  188 us
    reduce_scatter x1, waiting for transfers between devices, shards(): lax.psum_scatter(spread_rows(0, panel_size, slot_ids, live_count, mask_wo...  64 us
    psum x1, waiting for transfers between devices, shards(): grad_self, grad_neigh = lax.psum((grad_self, grad_neigh), ('row', 'col'))  39.2 us
    scatter-add x11, other arithmetic, spread_one_group(): return running.at[column_block - first_block].add(products)  35.2 us
    reduce_scatter x1, waiting for transfers between devices, shards(): lax.psum_scatter(partial_value.astype(jnp.bfloat16), 'col', scatter_dimen...  23.3 us
    gather x11, local copies, waits for them, and re-layouts, spread_one_group(): mask_words[chosen]  18.3 us
    gather x11, local copies, waits for them, and re-layouts, aggregate_one_group(): mask_words[chosen]  18.3 us
    scatter-add x11, other arithmetic, aggregate_one_group(): return shaped.at[row_block].add(products).reshape(running.shape)  14.7 us
  transfers between devices with their start and end apart: 10, of which 8 were waited for; matrix products, arithmetic and copies ran while one was open for 16% of the time, Pallas kernels for 0%

profile of v1, /device:TPU:0, one launch (start us, length us, event | category | flops | bytes accessed | tf_op | source)
XLA Modules:
  0.0 538.2 jit_solution(14736770928936795774)
XLA Ops:
  7.2 3.0 collective-permute-start
  10.3 6.7 %collective-permute-done = bf16[256,256]{1,0:T(8,128)(2,1)S(1)} collective-permute-done((bf16[256,256]{1,0:T(8,128)(2,1)}, bf16[256,256]{1,0:T(8,128)(2,1)S(1)}, u32[]{:S(2)}, u32[]{:S(2)}) %collective-permute-start) | collective-permute-done | bytes 131104 | tf_op jit(solution)/shard_map/ppermute | solution.py:117
  17.0 4.7 collective-permute-start.4
  21.7 2.9 collective-permute-done.1
  25.0 4.7 collective-permute-start.5
  29.7 2.7 collective-permute-done.2
  35.7 4.8 collective-permute-start.6
  44.4 253.3 %while.30 = (s32[]{:T(128)}, f32[1024,256]{1,0:T(8,128)S(1)}, s32[]{:T(128)}, s32[]{:T(128)}, s32[88]{0:T(128)S(1)}, /*index=5*/s32[88,16,128]{2,1,0:T(8,128)}, ...) while((s32[]{:T(128)}, f32[1024,256]{1,0:T(8,128)S(1)}, ...), condition=%wide.region_4.5_spmd.clone, body=%wide.region_2.4_spmd.clone.sunk | while | flops 67902872 | bytes 5061454 | solution.py:68
  45.8 17.3 %while.32 = (s32[]{:T(128)}, bf16[2304,256]{1,0:T(8,128)(2,1)}, s32[8,2]{0,1:T(2,128)S(1)}, bf16[8,128,256]{2,1,0:T(8,128)(2,1)S(1)}, s32[]{:T(128)}) while((s32[]{:T(128)}, bf16[2304,256]{1,0:T(8,128)(2,1)}, s32[8,2]{0,1:T(2,128)S(1)}, bf16[8,128,256]{2,1,0:T(8,128)(2,1)S(1)}, s32[]{:T(128)}) %tuple.84), condition=%wide.while_cond, body=%wide.while_body.sunk | while | flops 2 | bytes 131177 | solution.py:56
  46.4 1.6 bitcast_dynamic-update-slice_fusion.2
  48.6 1.6 bitcast_dynamic-update-slice_fusion.2
  50.7 1.6 bitcast_dynamic-update-slice_fusion.2
  52.9 1.6 bitcast_dynamic-update-slice_fusion.2
  63.9 1.7 gather_fusion.4
  68.8 17.3 %while.32 = (s32[]{:T(128)}, bf16[2304,256]{1,0:T(8,128)(2,1)}, s32[8,2]{0,1:T(2,128)S(1)}, bf16[8,128,256]{2,1,0:T(8,128)(2,1)S(1)}, s32[]{:T(128)}) while((s32[]{:T(128)}, bf16[2304,256]{1,0:T(8,128)(2,1)}, s32[8,2]{0,1:T(2,128)S(1)}, bf16[8,128,256]{2,1,0:T(8,128)(2,1)S(1)}, s32[]{:T(128)}) %tuple.84), condition=%wide.while_cond, body=%wide.while_body.sunk | while | flops 2 | bytes 131177 | solution.py:56
  86.9 1.7 gather_fusion.4
  91.9 17.3 %while.32 = (s32[]{:T(128)}, bf16[2304,256]{1,0:T(8,128)(2,1)}, s32[8,2]{0,1:T(2,128)S(1)}, bf16[8,128,256]{2,1,0:T(8,128)(2,1)S(1)}, s32[]{:T(128)}) while((s32[]{:T(128)}, bf16[2304,256]{1,0:T(8,128)(2,1)}, s32[8,2]{0,1:T(2,128)S(1)}, bf16[8,128,256]{2,1,0:T(8,128)(2,1)S(1)}, s32[]{:T(128)}) %tuple.84), condition=%wide.while_cond, body=%wide.while_body.sunk | while | flops 2 | bytes 131177 | solution.py:56
  110.0 1.7 gather_fusion.4
  114.9 17.3 %while.32 = (s32[]{:T(128)}, bf16[2304,256]{1,0:T(8,128)(2,1)}, s32[8,2]{0,1:T(2,128)S(1)}, bf16[8,128,256]{2,1,0:T(8,128)(2,1)S(1)}, s32[]{:T(128)}) while((s32[]{:T(128)}, bf16[2304,256]{1,0:T(8,128)(2,1)}, s32[8,2]{0,1:T(2,128)S(1)}, bf16[8,128,256]{2,1,0:T(8,128)(2,1)S(1)}, s32[]{:T(128)}) %tuple.84), condition=%wide.while_cond, body=%wide.while_body.sunk | while | flops 2 | bytes 131177 | solution.py:56
  133.0 1.7 gather_fusion.4
  137.9 17.3 %while.32 = (s32[]{:T(128)}, bf16[2304,256]{1,0:T(8,128)(2,1)}, s32[8,2]{0,1:T(2,128)S(1)}, bf16[8,128,256]{2,1,0:T(8,128)(2,1)S(1)}, s32[]{:T(128)}) while((s32[]{:T(128)}, bf16[2304,256]{1,0:T(8,128)(2,1)}, s32[8,2]{0,1:T(2,128)S(1)}, bf16[8,128,256]{2,1,0:T(8,128)(2,1)S(1)}, s32[]{:T(128)}) %tuple.84), condition=%wide.while_cond, body=%wide.while_body.sunk | while | flops 2 | bytes 131177 | solution.py:56
  156.0 1.7 gather_fusion.4
  161.0 17.3 %while.32 = (s32[]{:T(128)}, bf16[2304,256]{1,0:T(8,128)(2,1)}, s32[8,2]{0,1:T(2,128)S(1)}, bf16[8,128,256]{2,1,0:T(8,128)(2,1)S(1)}, s32[]{:T(128)}) while((s32[]{:T(128)}, bf16[2304,256]{1,0:T(8,128)(2,1)}, s32[8,2]{0,1:T(2,128)S(1)}, bf16[8,128,256]{2,1,0:T(8,128)(2,1)S(1)}, s32[]{:T(128)}) %tuple.84), condition=%wide.while_cond, body=%wide.while_body.sunk | while | flops 2 | bytes 131177 | solution.py:56
  179.1 1.7 gather_fusion.4
  184.0 17.3 %while.32 = (s32[]{:T(128)}, bf16[2304,256]{1,0:T(8,128)(2,1)}, s32[8,2]{0,1:T(2,128)S(1)}, bf16[8,128,256]{2,1,0:T(8,128)(2,1)S(1)}, s32[]{:T(128)}) while((s32[]{:T(128)}, bf16[2304,256]{1,0:T(8,128)(2,1)}, s32[8,2]{0,1:T(2,128)S(1)}, bf16[8,128,256]{2,1,0:T(8,128)(2,1)S(1)}, s32[]{:T(128)}) %tuple.84), condition=%wide.while_cond, body=%wide.while_body.sunk | while | flops 2 | bytes 131177 | solution.py:56
  202.1 1.7 gather_fusion.4
  207.0 17.3 %while.32 = (s32[]{:T(128)}, bf16[2304,256]{1,0:T(8,128)(2,1)}, s32[8,2]{0,1:T(2,128)S(1)}, bf16[8,128,256]{2,1,0:T(8,128)(2,1)S(1)}, s32[]{:T(128)}) while((s32[]{:T(128)}, bf16[2304,256]{1,0:T(8,128)(2,1)}, s32[8,2]{0,1:T(2,128)S(1)}, bf16[8,128,256]{2,1,0:T(8,128)(2,1)S(1)}, s32[]{:T(128)}) %tuple.84), condition=%wide.while_cond, body=%wide.while_body.sunk | while | flops 2 | bytes 131177 | solution.py:56
  225.1 1.7 gather_fusion.4
  230.0 17.3 %while.32 = (s32[]{:T(128)}, bf16[2304,256]{1,0:T(8,128)(2,1)}, s32[8,2]{0,1:T(2,128)S(1)}, bf16[8,128,256]{2,1,0:T(8,128)(2,1)S(1)}, s32[]{:T(128)}) while((s32[]{:T(128)}, bf16[2304,256]{1,0:T(8,128)(2,1)}, s32[8,2]{0,1:T(2,128)S(1)}, bf16[8,128,256]{2,1,0:T(8,128)(2,1)S(1)}, s32[]{:T(128)}) %tuple.84), condition=%wide.while_cond, body=%wide.while_body.sunk | while | flops 2 | bytes 131177 | solution.py:56
  248.1 1.7 gather_fusion.4
  253.1 17.3 %while.32 = (s32[]{:T(128)}, bf16[2304,256]{1,0:T(8,128)(2,1)}, s32[8,2]{0,1:T(2,128)S(1)}, bf16[8,128,256]{2,1,0:T(8,128)(2,1)S(1)}, s32[]{:T(128)}) while((s32[]{:T(128)}, bf16[2304,256]{1,0:T(8,128)(2,1)}, s32[8,2]{0,1:T(2,128)S(1)}, bf16[8,128,256]{2,1,0:T(8,128)(2,1)S(1)}, s32[]{:T(128)}) %tuple.84), condition=%wide.while_cond, body=%wide.while_body.sunk | while | flops 2 | bytes 131177 | solution.py:56
  271.2 1.7 gather_fusion.4
  276.1 17.3 %while.32 = (s32[]{:T(128)}, bf16[2304,256]{1,0:T(8,128)(2,1)}, s32[8,2]{0,1:T(2,128)S(1)}, bf16[8,128,256]{2,1,0:T(8,128)(2,1)S(1)}, s32[]{:T(128)}) while((s32[]{:T(128)}, bf16[2304,256]{1,0:T(8,128)(2,1)}, s32[8,2]{0,1:T(2,128)S(1)}, bf16[8,128,256]{2,1,0:T(8,128)(2,1)S(1)}, s32[]{:T(128)}) %tuple.84), condition=%wide.while_cond, body=%wide.while_body.sunk | while | flops 2 | bytes 131177 | solution.py:56
  294.2 1.7 gather_fusion.4
  299.0 23.3 %reduce-scatter.3.cloned.1.call-done = bf16[256,256]{1,0:T(8,128)(2,1)} async-done(((bf16[1024,256]{1,0:T(8,128)(2,1)}), bf16[256,256]{1,0:T(8,128)(2,1)}) %reduce-scatter.3.cloned.1.call-update) | async-done | bytes 131088 | tf_op jit(solution)/shard_map/reduce_scatter | solution.py:123
  322.3 2.0 multiply_convert_fusion
  325.4 6.6 %all_gather.3 = bf16[1024,256]{1,0:T(8,128)(2,1)S(1)} all-gather(bf16[256,256]{1,0:T(8,128)(2,1)S(1)} %fusion.42), channel_id=1, replica_groups=mesh['row'=8,'col'=4] {'col'}, dimensions={0}, use_global_device_ids=true | all-gather | bytes 655360 | tf_op jit(solution)/shard_map/all_gather | solution.py:149
  334.6 86.6 %while.31 = (s32[]{:T(128)}, f32[16,128,256]{2,1,0:T(8,128)}, s32[]{:T(128)}, s32[]{:T(128)}, s32[88]{0:T(128)S(1)}, /*index=5*/s32[88,16,128]{2,1,0:T(8,128)}, ...) while((s32[]{:T(128)}, f32[16,128,256]{2,1,0:T(8,128)}, s32[]{:T(128)}, ...), condition=%wide.region_8.9_spmd.clone, body=%wide.region_6.8_spmd.clone.sunk | while | flops 67897608 | bytes 5974609 | solution.py:101
  337.3 1.7 gather_fusion.2
  339.3 3.3 scatter_fusion
  345.2 1.7 gather_fusion.2
  347.3 3.2 scatter_fusion
  353.1 1.7 gather_fusion.2
  355.1 3.1 scatter_fusion
  360.9 1.7 gather_fusion.2
  362.9 3.2 scatter_fusion
  368.8 1.7 gather_fusion.2
  370.8 3.1 scatter_fusion
  376.6 1.7 gather_fusion.2
  378.6 3.1 scatter_fusion
  384.4 1.7 gather_fusion.2
  386.4 3.2 scatter_fusion
  392.3 1.7 gather_fusion.2
  394.3 3.4 scatter_fusion
  400.4 1.7 gather_fusion.2
  402.4 3.1 scatter_fusion
  408.2 1.7 gather_fusion.2
  410.2 3.1 scatter_fusion
  416.0 1.7 gather_fusion.2
  418.0 3.2 scatter_fusion
  421.2 2.7 convert_element_type.88
  423.9 39.2 %all-reduce.4.cloned.1.call-done = (f32[256,256]{0,1:T(8,128)}, f32[256,256]{0,1:T(8,128)}) async-done(((f32[256,256]{0,1:T(8,128)}, f32[256,256]{0,1:T(8,128)}), (f32[256,256]{0,1:T(8,128)}, f32[256,256]{0,1:T(8,128)})) %all-reduce.4.cloned.1.call-update) | async-done | bytes 524304 | tf_op jit(solution)/shard_map/psum | solution.py:143
  465.9 64.0 %reduce-scatter.5.cloned.1.call-done = bf16[256,256]{1,0:T(8,128)(2,1)} async-done(((bf16[2048,256]{1,0:T(8,128)(2,1)}), bf16[256,256]{1,0:T(8,128)(2,1)}) %reduce-scatter.5.cloned.1.call-update) | async-done | bytes 131088 | tf_op jit(solution)/shard_map/reduce_scatter | solution.py:151
  529.9 1.8 fusion.41
  (573 shorter events, 257.7 us)
Async XLA Ops:
  7.2 315.1 %copy-start = (bf16[256,256]{1,0:T(8,128)(2,1)S(1)}, bf16[256,256]{1,0:T(8,128)(2,1)}, u32[]{:S(2)}) copy-start(bf16[256,256]{1,0:T(8,128)(2,1)} %param.17) | copy-start | bytes 393220
  7.2 35.9 %copy-start.2 = (bf16[256,256]{1,0:T(8,128)(2,1)S(1)}, bf16[256,256]{1,0:T(8,128)(2,1)}, u32[]{:S(2)}) copy-start(bf16[256,256]{1,0:T(8,128)(2,1)} %param.13) | copy-start | bytes 393220
  7.2 315.1 %reduce-scatter.3.cloned.1.call-start = ((), (), s32[]{:S(2)}) async-start(), calls=%async_computation.2 | async-start | bytes 655360 | tf_op jit(solution)/shard_map/reduce_scatter | solution.py:123
  7.2 9.8 %collective-permute-start = (bf16[256,256]{1,0:T(8,128)(2,1)}, bf16[256,256]{1,0:T(8,128)(2,1)S(1)}, u32[]{:S(2)}, u32[]{:S(2)}) collective-permute-start(bf16[256,256]{1,0:T(8,128)(2,1)} %param.13), channel_id=1, source_target_pairs={{0,4},{4,8},{8,12},{12,16},{16,20},{20,24},{24,28},{28,0},{1,5},{5... | collective-permute-start | bytes 393224 | tf_op jit(solution)/shard_map/ppermute | solution.py:117
  17.0 7.7 %collective-permute-start.1 = (bf16[256,256]{1,0:T(8,128)(2,1)S(1)}, bf16[256,256]{1,0:T(8,128)(2,1)S(1)}, u32[]{:S(2)}, u32[]{:S(2)}) collective-permute-start(bf16[256,256]{1,0:T(8,128)(2,1)S(1)} %collective-permute-done), channel_id=1, source_target_pairs={{0,4},{4,8},{8,12},{12,16},{16,20},{20,24},{24,28},{28,0},{1,5},{5... | collective-permute-start | bytes 393224 | tf_op jit(solution)/shard_map/ppermute | solution.py:117
  17.0 8.0 %collective-permute-start.4 = (bf16[256,256]{1,0:T(8,128)(2,1)}, bf16[256,256]{1,0:T(8,128)(2,1)S(1)}, u32[]{:S(2)}, u32[]{:S(2)}) collective-permute-start(bf16[256,256]{1,0:T(8,128)(2,1)} %param.13), channel_id=1, source_target_pairs={{0,28},{4,0},{8,4},{12,8},{16,12},{20,16},{24,20},{28,24},{1,29},{... | collective-permute-start | bytes 393224 | tf_op jit(solution)/shard_map/ppermute | solution.py:119
  24.7 7.7 %collective-permute-start.2 = (bf16[256,256]{1,0:T(8,128)(2,1)S(1)}, bf16[256,256]{1,0:T(8,128)(2,1)S(1)}, u32[]{:S(2)}, u32[]{:S(2)}) collective-permute-start(bf16[256,256]{1,0:T(8,128)(2,1)S(1)} %collective-permute-done.1), channel_id=1, source_target_pairs={{0,4},{4,8},{8,12},{12,16},{16,20},{20,24},{24,28},{28,0},{1,5},{5... | collective-permute-start | bytes 393224 | tf_op jit(solution)/shard_map/ppermute | solution.py:117
  25.0 10.7 %collective-permute-start.5 = (bf16[256,256]{1,0:T(8,128)(2,1)S(1)}, bf16[256,256]{1,0:T(8,128)(2,1)S(1)}, u32[]{:S(2)}, u32[]{:S(2)}) collective-permute-start(bf16[256,256]{1,0:T(8,128)(2,1)S(1)} %collective-permute-done.4), channel_id=1, source_target_pairs={{0,28},{4,0},{8,4},{12,8},{16,12},{20,16},{24,20},{28,24},{1,29},{... | collective-permute-start | bytes 393224 | tf_op jit(solution)/shard_map/ppermute | solution.py:119
  32.4 8.1 %collective-permute-start.3 = (bf16[256,256]{1,0:T(8,128)(2,1)S(1)}, bf16[256,256]{1,0:T(8,128)(2,1)S(1)}, u32[]{:S(2)}, u32[]{:S(2)}) collective-permute-start(bf16[256,256]{1,0:T(8,128)(2,1)S(1)} %collective-permute-done.2), channel_id=1, source_target_pairs={{0,4},{4,8},{8,12},{12,16},{16,20},{20,24},{24,28},{28,0},{1,5},{5... | collective-permute-start | bytes 393224 | tf_op jit(solution)/shard_map/ppermute | solution.py:117
  35.7 7.3 %collective-permute-start.6 = (bf16[256,256]{1,0:T(8,128)(2,1)S(1)}, bf16[256,256]{1,0:T(8,128)(2,1)S(1)}, u32[]{:S(2)}, u32[]{:S(2)}) collective-permute-start(bf16[256,256]{1,0:T(8,128)(2,1)S(1)} %collective-permute-done.5), channel_id=1, source_target_pairs={{0,28},{4,0},{8,4},{12,8},{16,12},{20,16},{24,20},{28,24},{1,29},{... | collective-permute-start | bytes 393224 | tf_op jit(solution)/shard_map/ppermute | solution.py:119
  43.2 1.2 copy-start.1
  297.8 1.0 copy-start.4
  297.8 1.0 copy-start.3
  297.8 24.5 %copy-start.5 = (bf16[256,256]{1,0:T(8,128)(2,1)S(1)}, bf16[256,256]{1,0:T(8,128)(2,1)}, u32[]{:S(2)}) copy-start(bf16[256,256]{1,0:T(8,128)(2,1)} %param.14) | copy-start | bytes 393220
  297.8 24.5 %copy-start.7 = (f32[256]{0:T(256)S(1)}, f32[256]{0:T(256)}, u32[]{:S(2)}) copy-start(f32[256]{0:T(256)} %param.18) | copy-start | bytes 3076
  298.7 164.5 %all-reduce.4.cloned.1.call-start = ((), (), s32[]{:S(2)}) async-start(), calls=%async_computation.4 | async-start | bytes 1048576 | tf_op jit(solution)/shard_map/psum | solution.py:143
  322.3 9.7 %copy-start.6 = (bf16[256,256]{1,0:T(8,128)(2,1)S(1)}, bf16[256,256]{1,0:T(8,128)(2,1)}, u32[]{:S(2)}) copy-start(bf16[256,256]{1,0:T(8,128)(2,1)} %reduce-scatter.3.cloned.1.call-done) | copy-start | bytes 393220
  333.1 196.8 %reduce-scatter.5.cloned.1.call-start = ((), (), s32[]{:S(2)}) async-start(), calls=%async_computation.3 | async-start | bytes 1179648 | tf_op jit(solution)/shard_map/reduce_scatter | solution.py:151
Sparse Core Ops, SparseCore 0:
  298.8 23.4 reduce-scatter.2
  333.2 129.9 all-reduce.3
  466.6 63.2 reduce-scatter.4
